TPU v7x, 256 devices: a whole 4x4x8 slice. The times are simulated.
256 devices in a mesh: seq: 32 (over x_hi, z, core), ch: 8 (over y, x_lo).
Axes of the slice: x: 4 (x_hi: 2, x_lo: 2; x = x_hi * 2 + x_lo), y: 4, z: 8, core: 2. Of those that a mesh axis runs over, the one named last changes fastest.
Arguments:
- hidden: bfloat16 [4096, 2048], P('seq', 'ch'), may hold values from -400 to 400, as said below
- tokens: int32 [4096], replicated, may hold values from 0 to 3
- edit_bounds: int32 [8, 2], replicated, may hold values from 0 to 4095
- norm_gain: float32 [2048], replicated, may hold values from 0.1 to 1.9
- base_embed: float32 [4, 2048], replicated, may hold values from -6 to 6
- w_in: bfloat16 [2, 2048, 4096], P(None, None, 'ch'), may hold values from -0.125 to 0.125
- conv_w: float32 [4, 4096], P(None, 'ch'), may hold values from -3 to 3
- conv_b: float32 [4096], P('ch'), may hold values from -3 to 3
- proj_bc: bfloat16 [32, 4096], P(None, 'ch'), may hold values from -0.1875 to 0.1875
- decay_rate: float32 [16, 4096], P(None, 'ch'), may hold values from 9.765625e-06 to 0.11, as said below
- skip_gain: float32 [4096], P('ch'), may hold values from -4 to 4
- w_out: bfloat16 [4096, 2048], P('ch'), may hold values from -0.09375 to 0.09375
Outputs:
- mixed: bfloat16 [4096, 2048], P('seq', 'ch')
Inputs may be any that keep to these rules, and one draw needn't show every extreme that they name: The hidden states have row and column scales that differ. `decay_rate`: each entry is a positive decay rate per position. `edit_bounds`: positions in the window; a span's start and end come in no fixed order and may coincide with others.
All inputs are finite; a program needn't handle non-finite values.
Results may differ from a plain program's by a relative error of at most 0.014.
Values may be sent and summed in bfloat16 or wider, within the bound.
A program may use at most 64 MiB of HBM per device.

v0:
```python
import jax
import jax.numpy as jnp
from jax import lax
from jax.sharding import PartitionSpec as P

CONV = 4
epsilon = 1e-05


def from_partner(block, axis, apart):
    count = lax.axis_size(axis)
    route = []
    for low in range(count):
        high = low | 1 << apart
        if high != low and high < count:
            route += [(low, high), (high, low)]
    return lax.ppermute(block, axis, route)


def passed_along(block, axis, distance):
    devices = range(lax.axis_size(axis))
    route = [(i - distance, i) for i in devices if i - distance in devices]
    return lax.ppermute(block, axis, route)


def carried_in(part, axis, combine, identity):
    place = lax.axis_index(axis)
    gathered = jax.tree.map(lambda a: lax.all_gather(a, axis), part)
    state = jax.tree.map(lambda a, e: jnp.zeros_like(a) + jnp.asarray(e, a.dtype), part, identity)

    def one(step, state):
        return combine(
            state, jax.tree.map(lambda a: lax.dynamic_index_in_dim(a, step, 0, False), gathered)
        )

    return lax.fori_loop(0, place, one, state)


def link(before, follow):
    return (before[0] * follow[0], before[1] * follow[0] + follow[1])


def link_pair(before, follow):
    return link(before[0:2], follow[0:2]) + link(before[2:4], follow[2:4])


def keep_rows(places, edit_bounds):
    hit_count = jnp.sum(
        (places[:, None] == edit_bounds.reshape(-1)[None, :]).astype(jnp.float32), axis=1
    )
    return 1.0 / (1.0 + hit_count)


def norm_rows(rows, bases, norm_gain, base_embed):
    row_values = rows.astype(jnp.float32)
    inv_rms = lax.rsqrt(jnp.mean(row_values * row_values, axis=1, keepdims=True) + epsilon)
    one_hot = (bases[:, None] == jnp.arange(4, dtype=jnp.int32)[None, :]).astype(jnp.float32)
    embedded = one_hot[:, 0:1] * base_embed[0][None, :]
    for base_index in range(1, 4):
        embedded = (
            embedded + one_hot[:, base_index : base_index + 1] * base_embed[base_index][None, :]
        )
    return (row_values * inv_rms * norm_gain[None, :] + embedded).astype(jnp.bfloat16)


def run_chain(
    start_state, keep_both, inputs_b, inputs_r, mixed_both, decay_mult, drive_gain, want_rows
):
    row_count = mixed_both.shape[1]
    inner_width = mixed_both.shape[2]
    state_size = inputs_b.shape[1]
    turns = 8
    per_turn = row_count // turns
    keep_blocks = keep_both.T.reshape(turns, per_turn, 2)
    b_blocks = inputs_b.transpose(2, 0, 1).reshape(turns, per_turn, 2, state_size)
    r_blocks = inputs_r.transpose(2, 0, 1).reshape(turns, per_turn, 2, state_size)
    x_blocks = mixed_both.transpose(1, 0, 2).reshape(turns, per_turn, 2, inner_width)

    def turn_step(state, block):
        keep_block, b_block, r_block, x_block = block
        outputs = []
        for row_index in range(per_turn):
            x_float = x_block[row_index].astype(jnp.float32)
            state = (
                keep_block[row_index][:, None, None] * decay_mult[None] * state
                + drive_gain[None] * b_block[row_index][:, :, None] * x_float[:, None, :]
            )
            if want_rows:
                outputs.append(jnp.sum(r_block[row_index][:, :, None] * state, axis=1))
        if want_rows:
            return (state, jnp.stack(outputs))
        return (state, jnp.zeros((), jnp.float32))

    final_state, produced = lax.scan(
        turn_step, start_state, (keep_blocks, b_blocks, r_blocks, x_blocks)
    )
    if want_rows:
        return (final_state, produced.reshape(row_count, 2, inner_width).transpose(1, 0, 2))
    return (final_state, None)


def body(
    hidden,
    tokens,
    edit_bounds,
    norm_gain,
    base_embed,
    w_in,
    conv_w,
    conv_b,
    proj_bc,
    decay_rate,
    skip_gain,
    w_out,
):
    row_count = hidden.shape[0]
    seq_count = lax.axis_size("seq")
    where_am = lax.axis_index("seq")
    levels = seq_count.bit_length() - 1
    own_bases = lax.dynamic_slice_in_dim(tokens, where_am * row_count, row_count)
    partner_shard = hidden
    for bit_index in range(levels):
        partner_shard = from_partner(partner_shard, "seq", bit_index)
    owner_dev = seq_count - 1 - where_am
    to_gather = jnp.stack([hidden, partner_shard])
    gathered = lax.all_gather(to_gather, "ch", axis=2, tiled=True)
    normed = norm_rows(gathered[0], own_bases, norm_gain, base_embed)
    far_bases = lax.dynamic_slice_in_dim(tokens, owner_dev * row_count, row_count)
    partner = norm_rows(gathered[1], far_bases, norm_gain, base_embed)
    offsets = jnp.arange(row_count, dtype=jnp.int32)
    keep_ahead = keep_rows(where_am * row_count + offsets, edit_bounds)
    back_rows = partner[::-1, ::-1]
    keep_back = keep_rows(owner_dev * row_count + row_count - 1 - offsets, edit_bounds)
    stacked = jnp.concatenate([normed, back_rows], axis=0)
    both_proj = lax.dot_general(
        stacked, w_in, (((1,), (1,)), ((), ())), preferred_element_type=jnp.float32
    ).astype(jnp.bfloat16)
    x_part = both_proj[:, 0, :].reshape(2, row_count, -1)
    z_part = both_proj[:, 1, :].reshape(2, row_count, -1)
    rims = x_part[:, row_count - CONV + 1 :, :]
    rims_in = passed_along(rims, "seq", 1)
    padded = jnp.concatenate([rims_in, x_part], axis=1)
    conv_sum = conv_b[None, None, :] + jnp.zeros(x_part.shape, jnp.float32)
    for tap_index in range(CONV):
        conv_sum = (
            conv_sum
            + padded[:, tap_index : tap_index + row_count, :].astype(jnp.float32)
            * conv_w[tap_index][None, None, :]
        )
    mixed_in = jax.nn.silu(conv_sum).astype(jnp.bfloat16)
    partial_bc = jnp.einsum("kc,slc->skl", proj_bc, mixed_in, preferred_element_type=jnp.float32)
    inputs_bc = lax.psum(partial_bc, "ch")
    state_size = decay_rate.shape[0]
    inputs_b = inputs_bc[:, :state_size]
    inputs_r = inputs_bc[:, state_size:]
    decay_mult = jnp.exp(-decay_rate)
    drive_gain = jnp.sqrt(-jnp.expm1(-2.0 * decay_rate))
    keep_both = jnp.stack([keep_ahead, keep_back])
    zero_state = jnp.zeros((2,) + decay_rate.shape, jnp.float32)
    local_end, unused = run_chain(
        zero_state, keep_both, inputs_b, inputs_r, mixed_in, decay_mult, drive_gain, False
    )
    block_decay = jnp.exp(-float(row_count) * decay_rate)
    pass_ahead = jnp.prod(keep_ahead) * block_decay
    pass_back = jnp.prod(keep_back) * block_decay
    identity_pair = (jnp.ones_like(decay_mult), jnp.zeros_like(decay_mult))
    carried = carried_in(
        (pass_ahead, local_end[0], pass_back, local_end[1]),
        "seq",
        link_pair,
        identity_pair + identity_pair,
    )
    carry_fore = carried[1]
    carry_aft = carried[3]
    entering = jnp.stack([carry_fore, carry_aft])
    final_unused, read_rows = run_chain(
        entering, keep_both, inputs_b, inputs_r, mixed_in, decay_mult, drive_gain, True
    )
    y_out = read_rows + skip_gain[None, None, :] * mixed_in.astype(jnp.float32)
    gated = (y_out * jax.nn.silu(z_part.astype(jnp.float32))).astype(jnp.bfloat16)
    gated_ahead = gated[0]
    gated_back = gated[1]
    for bit_index in range(levels):
        gated_back = from_partner(gated_back, "seq", bit_index)
    aligned = gated_back[::-1]
    summed = (
        jnp.dot(gated_ahead, w_out, preferred_element_type=jnp.float32)
        + jnp.dot(aligned, w_out, preferred_element_type=jnp.float32)[:, ::-1]
    )
    return lax.psum_scatter(summed.astype(jnp.bfloat16), "ch", scatter_dimension=1, tiled=True)


def solution(mesh):
    placed = (
        P("seq", "ch"),
        P(),
        P(),
        P(),
        P(),
        P(None, None, "ch"),
        P(None, "ch"),
        P("ch"),
        P(None, "ch"),
        P(None, "ch"),
        P("ch"),
        P("ch", None),
    )
    return jax.shard_map(
        body, mesh=mesh, in_specs=placed, out_specs=P("seq", "ch"), check_vma=False
    )
```

profile of v0, /device:TPU:4, one launch (start us, length us, event | category | flops | bytes accessed | tf_op | source)
XLA Modules:
  0.0 528.3 jit_solution(1080955099993510452)
XLA Ops:
  6.5 1.5 collective-permute-done
  8.0 1.9 collective-permute-start.1
  9.9 2.4 collective-permute-done.1
  12.3 3.3 collective-permute-start.2
  15.6 2.6 collective-permute-done.2
  18.2 7.3 %collective-permute-start.3 = (bf16[128,256]{1,0:T(8,128)(2,1)S(1)}, bf16[128,256]{1,0:T(8,128)(2,1)S(1)}, u32[]{:S(2)}, u32[]{:S(2)}) collective-permute-start(bf16[128,256]{1,0:T(8,128)(2,1)S(1)} %collective-permute-done.2), channel_id=1, source_target_pairs={{0,64},{64,0},{8,72},{72,8},{16,80},{80,16},{24,88},{88,24},{32,96... | collective-permute-start | bytes 196616 | tf_op jit(solution)/shard_map/ppermute | solution.py:17
  25.4 2.3 collective-permute-done.3
  27.7 1.5 collective-permute-start.4
  29.2 4.2 collective-permute-done.4
  33.5 1.5 pad_maximum_fusion.1
  35.0 0.8 copy.37
  36.0 0.7 fusion.192
  36.7 2.6 fusion.187
  39.4 0.7 all-gather.14.cloned.1.call-update
  40.1 0.8 fusion.197
  40.9 0.9 fusion.196
  41.9 0.9 fusion.198
  42.7 36.3 %all-gather.8.cloned.1.call-done = bf16[2,128,2048]{2,1,0:T(8,128)(2,1)} async-done(((bf16[2,128,256]{2,1,0:T(8,128)(2,1)}), bf16[2,128,2048]{2,1,0:T(8,128)(2,1)}) %all-gather.8.cloned.1.call-update) | async-done | bytes 1048592 | tf_op jit(solution)/shard_map/all_gather | solution.py:126
  79.0 1.5 fusion.168
  80.5 2.9 fusion.171
  83.5 1.8 rev.9
  85.3 3.6 convolution_convert_fusion
  89.0 1.9 collective-permute-start.5
  91.0 6.5 %collective-permute-done.5 = bf16[2,3,512]{2,1,0:T(4,128)(2,1)S(1)} collective-permute-done((bf16[2,3,512]{2,1,0:T(4,128)(2,1)S(1)}, bf16[2,3,512]{2,1,0:T(4,128)(2,1)S(1)}, u32[]{:S(2)}, u32[]{:S(2)}) %collective-permute-start.5) | collective-permute-done | bytes 6176 | tf_op jit(solution)/shard_map/ppermute | solution.py:23
  98.4 34.0 %psum.7 = f32[2,32,128]{2,1,0:T(8,128)S(1)} all-reduce(f32[2,32,128]{2,1,0:T(8,128)S(1)} %convolution_bitcast_fusion), channel_id=1, replica_groups=mesh['seq'=32,'ch'=8] {'ch'}, use_global_device_ids=true, to_apply=%region_5.6 | all-reduce | flops 8192 | bytes 65536 | tf_op jit(solution)/shard_map/psum | solution.py:152
  132.5 5.1 while.41
  139.0 20.7 %all-gather.16.cloned.1.call-done = f32[512,512]{1,0:T(8,128)} async-done(((f32[16,512]{1,0:T(8,128)}), f32[512,512]{1,0:T(8,128)}) %all-gather.16.cloned.1.call-update) | async-done | bytes 1048592 | tf_op jit(solution)/shard_map/all_gather | solution.py:28
  159.7 77.5 %all-gather.14.cloned.1.call-done = f32[512,512]{1,0:T(8,128)} async-done(((f32[16,512]{1,0:T(8,128)}), f32[512,512]{1,0:T(8,128)}) %all-gather.14.cloned.1.call-update) | async-done | bytes 1048592 | tf_op jit(solution)/shard_map/all_gather | solution.py:28
  237.2 77.3 %all-gather.10.cloned.1.call-done = f32[32,16,512]{2,1,0:T(8,128)} async-done(((f32[1,16,512]{2,1,0:T(8,128)}), f32[32,16,512]{2,1,0:T(8,128)}) %all-gather.10.cloned.1.call-update) | async-done | bytes 1048592 | tf_op jit(solution)/shard_map/all_gather | solution.py:28
  314.5 77.3 %all-gather.12.cloned.1.call-done = f32[32,16,512]{2,1,0:T(8,128)} async-done(((f32[1,16,512]{2,1,0:T(8,128)}), f32[32,16,512]{2,1,0:T(8,128)}) %all-gather.12.cloned.1.call-update) | async-done | bytes 1048592 | tf_op jit(solution)/shard_map/all_gather | solution.py:28
  391.8 13.8 %while.39 = (s32[]{:T(128)}, f32[16,512]{1,0:T(8,128)S(1)}, f32[16,512]{1,0:T(8,128)S(1)}, s32[]{:T(128)}, f32[32,16,512]{2,1,0:T(8,128)}, /*index=5*/f32[32,16,...) while((s32[]{:T(128)}, f32[16,512]{1,0:T(8,128)S(1)}, ...), condition=%wide.region_10.11_spmd, body=%wide.region_9.10_spmd.sunk | while | flops 32773 | bytes 262291 | solution.py:36
  391.8 0.8 bitcast_add_fusion.4
  392.7 0.8 bitcast_add_fusion.4
  393.6 0.8 bitcast_add_fusion.4
  394.4 0.8 bitcast_add_fusion.4
  395.3 0.8 bitcast_add_fusion.4
  396.2 0.8 bitcast_add_fusion.4
  397.0 0.8 bitcast_add_fusion.4
  397.9 0.8 bitcast_add_fusion.4
  398.8 0.8 bitcast_add_fusion.4
  399.6 0.8 bitcast_add_fusion.4
  400.5 0.8 bitcast_add_fusion.4
  401.4 0.8 bitcast_add_fusion.4
  402.2 0.8 bitcast_add_fusion.4
  403.1 0.8 bitcast_add_fusion.4
  404.0 0.8 bitcast_add_fusion.4
  404.8 0.8 bitcast_add_fusion.4
  405.7 16.8 %while.40 = (s32[]{:T(128)}, f32[2,16,512]{2,1,0:T(8,128)S(1)}, f32[8,16,2,512]{3,2,1,0:T(2,128)}, f32[8,16,2]{2,1,0:T(8,128)S(1)}, f32[16,512]{1,0:T(8,128)S(1)...) while((s32[]{:T(128)}, f32[2,16,512]{2,1,0:T(8,128)S(1)}, ...), condition=%wide.region_28.29_spmd, body=%wide.region_11.28_spmd.sunk | while | flops 2818065 | bytes 1473593 | solution.py:94
  407.3 0.6 bitcast_dynamic-update-slice_fusion.2
  417.7 0.6 bitcast_dynamic-update-slice_fusion.2
  422.5 1.2 fusion.182
  423.7 1.2 collective-permute-start.6
  424.9 1.0 collective-permute-done.6
  425.9 2.6 collective-permute-start.7
  428.5 4.0 collective-permute-done.7
  432.5 6.1 %collective-permute-start.8 = (bf16[128,512]{1,0:T(8,128)(2,1)S(1)}, bf16[128,512]{1,0:T(8,128)(2,1)S(1)}, u32[]{:S(2)}, u32[]{:S(2)}) collective-permute-start(bf16[128,512]{1,0:T(8,128)(2,1)S(1)} %collective-permute-done.7), channel_id=1, source_target_pairs={{0,32},{32,0},{8,40},{40,8},{16,48},{48,16},{24,56},{56,24},{64,96... | collective-permute-start | bytes 393224 | tf_op jit(solution)/shard_map/ppermute | solution.py:17
  438.6 6.3 %collective-permute-done.8 = bf16[128,512]{1,0:T(8,128)(2,1)S(1)} collective-permute-done((bf16[128,512]{1,0:T(8,128)(2,1)S(1)}, bf16[128,512]{1,0:T(8,128)(2,1)S(1)}, u32[]{:S(2)}, u32[]{:S(2)}) %collective-permute-start.8) | collective-permute-done | bytes 131104 | tf_op jit(solution)/shard_map/ppermute | solution.py:17
  444.9 8.6 %collective-permute-start.9 = (bf16[128,512]{1,0:T(8,128)(2,1)S(1)}, bf16[128,512]{1,0:T(8,128)(2,1)S(1)}, u32[]{:S(2)}, u32[]{:S(2)}) collective-permute-start(bf16[128,512]{1,0:T(8,128)(2,1)S(1)} %collective-permute-done.8), channel_id=1, source_target_pairs={{0,64},{64,0},{8,72},{72,8},{16,80},{80,16},{24,88},{88,24},{32,96... | collective-permute-start | bytes 393224 | tf_op jit(solution)/shard_map/ppermute | solution.py:17
  453.5 4.9 collective-permute-done.9
  458.9 6.0 %collective-permute-done.10 = bf16[128,512]{1,0:T(8,128)(2,1)S(1)} collective-permute-done((bf16[128,512]{1,0:T(8,128)(2,1)S(1)}, bf16[128,512]{1,0:T(8,128)(2,1)S(1)}, u32[]{:S(2)}, u32[]{:S(2)}) %collective-permute-start.10) | collective-permute-done | bytes 131104 | tf_op jit(solution)/shard_map/ppermute | solution.py:17
  465.1 1.5 fusion.199
  466.6 9.3 %rev.11 = f32[128,2048]{1,0:T(8,128)} reverse(f32[128,2048]{1,0:T(8,128)} %fusion.199), dimensions={1} | reverse | bytes 2097152 | tf_op jit(solution)/shard_map/rev | solution.py:188
  475.9 2.1 add_convert_fusion
  478.1 43.4 %reduce-scatter.2.cloned.1.call-done = bf16[128,256]{1,0:T(8,128)(2,1)} async-done(((bf16[128,2048]{1,0:T(8,128)(2,1)}), bf16[128,256]{1,0:T(8,128)(2,1)}) %reduce-scatter.2.cloned.1.call-update) | async-done | bytes 65552 | tf_op jit(solution)/shard_map/reduce_scatter | solution.py:190
  (278 shorter events, 22.9 us)
Async XLA Ops:
  6.5 451.9 %copy-start = (bf16[512,2048]{1,0:T(8,128)(2,1)S(1)}, bf16[512,2048]{1,0:T(8,128)(2,1)}, u32[]{:S(2)}) copy-start(bf16[512,2048]{1,0:T(8,128)(2,1)} %param.29) | copy-start | bytes 6291460
  6.5 72.5 %all-gather.8.cloned.1.call-start = ((), (), s32[]{:S(2)}) async-start(), calls=%async_computation.1 | async-start | bytes 1179648 | tf_op jit(solution)/shard_map/all_gather | solution.py:126
  6.5 1.5 collective-permute-start
  8.0 4.3 collective-permute-start.1
  12.3 5.8 %collective-permute-start.2 = (bf16[128,256]{1,0:T(8,128)(2,1)S(1)}, bf16[128,256]{1,0:T(8,128)(2,1)S(1)}, u32[]{:S(2)}, u32[]{:S(2)}) collective-permute-start(bf16[128,256]{1,0:T(8,128)(2,1)S(1)} %collective-permute-done.1), channel_id=1, source_target_pairs={{0,32},{32,0},{8,40},{40,8},{16,48},{48,16},{24,56},{56,24},{64,96... | collective-permute-start | bytes 196616 | tf_op jit(solution)/shard_map/ppermute | solution.py:17
  18.2 9.5 %collective-permute-start.3 = (bf16[128,256]{1,0:T(8,128)(2,1)S(1)}, bf16[128,256]{1,0:T(8,128)(2,1)S(1)}, u32[]{:S(2)}, u32[]{:S(2)}) collective-permute-start(bf16[128,256]{1,0:T(8,128)(2,1)S(1)} %collective-permute-done.2), channel_id=1, source_target_pairs={{0,64},{64,0},{8,72},{72,8},{16,80},{80,16},{24,88},{88,24},{32,96... | collective-permute-start | bytes 196616 | tf_op jit(solution)/shard_map/ppermute | solution.py:17
  27.7 5.8 %collective-permute-start.4 = (bf16[128,256]{1,0:T(8,128)(2,1)S(1)}, bf16[128,256]{1,0:T(8,128)(2,1)S(1)}, u32[]{:S(2)}, u32[]{:S(2)}) collective-permute-start(bf16[128,256]{1,0:T(8,128)(2,1)S(1)} %collective-permute-done.3), channel_id=1, source_target_pairs={{0,128},{128,0},{8,136},{136,8},{16,144},{144,16},{24,152},{152,24... | collective-permute-start | bytes 196616 | tf_op jit(solution)/shard_map/ppermute | solution.py:17
  35.0 124.7 %all-gather.16.cloned.1.call-start = ((), (), s32[]{:S(2)}) async-start(), calls=%async_computation.6 | async-start | bytes 1081344 | tf_op jit(solution)/shard_map/all_gather | solution.py:28
  39.3 197.9 %all-gather.14.cloned.1.call-start = ((), (), s32[]{:S(2)}) async-start(), calls=%async_computation.5 | async-start | bytes 1081344 | tf_op jit(solution)/shard_map/all_gather | solution.py:28
  40.1 274.4 %all-gather.10.cloned.1.call-start = ((), (), s32[]{:S(2)}) async-start(), calls=%async_computation.2 | async-start | bytes 1081344 | tf_op jit(solution)/shard_map/all_gather | solution.py:28
  85.3 12.3 %copy-start.2 = (f32[512]{0:T(512)S(1)}, f32[512]{0:T(512)}, u32[]{:S(2)}) copy-start(f32[512]{0:T(512)} %param.25) | copy-start | bytes 6148
  88.9 9.3 %copy-start.1 = (bf16[32,512]{1,0:T(8,128)(2,1)S(1)}, bf16[32,512]{1,0:T(8,128)(2,1)}, u32[]{:S(2)}) copy-start(bf16[32,512]{1,0:T(8,128)(2,1)} %param.26) | copy-start | bytes 98308
  89.0 8.6 %collective-permute-start.5 = (bf16[2,3,512]{2,1,0:T(4,128)(2,1)S(1)}, bf16[2,3,512]{2,1,0:T(4,128)(2,1)S(1)}, u32[]{:S(2)}, u32[]{:S(2)}) collective-permute-start(bf16[2,3,512]{2,1,0:T(4,128)(2,1)S(1)} %slice.623), channel_id=1, source_target_pairs={{0,8},{8,16},{16,24},{24,32},{32,40},{40,48},{48,56},{56,64},{64,7... | collective-permute-start | bytes 18440 | tf_op jit(solution)/shard_map/ppermute | solution.py:23
  138.3 253.6 %all-gather.12.cloned.1.call-start = ((), (), s32[]{:S(2)}) async-start(), calls=%async_computation.3 | async-start | bytes 1081344 | tf_op jit(solution)/shard_map/all_gather | solution.py:28
  138.9 382.6 %reduce-scatter.2.cloned.1.call-start = ((), (), s32[]{:S(2)}) async-start(), calls=%async_computation.4 | async-start | bytes 589824 | tf_op jit(solution)/shard_map/reduce_scatter | solution.py:190
  405.7 16.8 %copy-start.3 = (f32[512]{0:T(512)S(1)}, f32[512]{0:T(512)}, u32[]{:S(2)}) copy-start(f32[512]{0:T(512)} %param.28) | copy-start | bytes 6148
  423.7 2.2 collective-permute-start.6
  425.9 6.7 %collective-permute-start.7 = (bf16[128,512]{1,0:T(8,128)(2,1)S(1)}, bf16[128,512]{1,0:T(8,128)(2,1)S(1)}, u32[]{:S(2)}, u32[]{:S(2)}) collective-permute-start(bf16[128,512]{1,0:T(8,128)(2,1)S(1)} %collective-permute-done.6), channel_id=1, source_target_pairs={{0,16},{16,0},{8,24},{24,8},{32,48},{48,32},{40,56},{56,40},{64,80... | collective-permute-start | bytes 393224 | tf_op jit(solution)/shard_map/ppermute | solution.py:17
  432.5 12.4 %collective-permute-start.8 = (bf16[128,512]{1,0:T(8,128)(2,1)S(1)}, bf16[128,512]{1,0:T(8,128)(2,1)S(1)}, u32[]{:S(2)}, u32[]{:S(2)}) collective-permute-start(bf16[128,512]{1,0:T(8,128)(2,1)S(1)} %collective-permute-done.7), channel_id=1, source_target_pairs={{0,32},{32,0},{8,40},{40,8},{16,48},{48,16},{24,56},{56,24},{64,96... | collective-permute-start | bytes 393224 | tf_op jit(solution)/shard_map/ppermute | solution.py:17
  444.9 13.5 %collective-permute-start.9 = (bf16[128,512]{1,0:T(8,128)(2,1)S(1)}, bf16[128,512]{1,0:T(8,128)(2,1)S(1)}, u32[]{:S(2)}, u32[]{:S(2)}) collective-permute-start(bf16[128,512]{1,0:T(8,128)(2,1)S(1)} %collective-permute-done.8), channel_id=1, source_target_pairs={{0,64},{64,0},{8,72},{72,8},{16,80},{80,16},{24,88},{88,24},{32,96... | collective-permute-start | bytes 393224 | tf_op jit(solution)/shard_map/ppermute | solution.py:17
  458.4 6.5 %collective-permute-start.10 = (bf16[128,512]{1,0:T(8,128)(2,1)S(1)}, bf16[128,512]{1,0:T(8,128)(2,1)S(1)}, u32[]{:S(2)}, u32[]{:S(2)}) collective-permute-start(bf16[128,512]{1,0:T(8,128)(2,1)S(1)} %collective-permute-done.9), channel_id=1, source_target_pairs={{0,128},{128,0},{8,136},{136,8},{16,144},{144,16},{24,152},{152,24... | collective-permute-start | bytes 393224 | tf_op jit(solution)/shard_map/ppermute | solution.py:17
Sparse Core Ops, SparseCore 0:
  35.1 43.8 all-gather.7
  81.8 77.8 all-gather.15
  162.5 74.6 all-gather.13
  239.8 74.5 all-gather.9
  317.1 74.6 all-gather.11
  478.2 43.2 reduce-scatter.1
where the time goes:
time: 532 us; the launch traced here: 528 us
  waiting for transfers between devices  375 us (70%)
  other arithmetic  38.7 us (7%)
  starting transfers between devices  34.7 us (7%)
  blocking collectives  34 us (6%)
  local copies, waits for them, and re-layouts  24.6 us (5%)
  between operations  13.7 us (3%)
  matrix products  5.68 us (1%)
    all_gather x4, waiting for transfers between devices, carried_in(): gathered = jax.tree.map(lambda a: lax.all_gather(a, axis), part)  253 us
    reduce_scatter x1, waiting for transfers between devices, body(): lax.psum_scatter(summed.astype(jnp.bfloat16), 'ch', scatter_dimension=1,...  43.4 us
    all_gather x1, waiting for transfers between devices, body(): gathered = lax.all_gather(to_gather, 'ch', axis=2, tiled=True)  36.3 us
    ppermute x10, waiting for transfers between devices, from_partner(): return lax.ppermute(block, axis, route)  35.1 us
    psum x1, blocking collectives, body(): inputs_bc = lax.psum(partial_bc, 'ch')  34 us
    ppermute x10, starting transfers between devices, from_partner(): return lax.ppermute(block, axis, route)  32.5 us
    add x16, other arithmetic, link(): return (before[0] * follow[0], before[1] * follow[0] + follow[1])  13.5 us
  transfers between devices with their start and end apart: 17, of which 17 were waited for; matrix products, arithmetic and copies ran while one was open for 4% of the time, Pallas kernels for 0%

commit v1 on v0

--- a/solution.py
+++ b/solution.py
@@ -149,7 +149,7 @@
         )
     mixed_in = jax.nn.silu(conv_sum).astype(jnp.bfloat16)
     partial_bc = jnp.einsum("kc,slc->skl", proj_bc, mixed_in, preferred_element_type=jnp.float32)
-    inputs_bc = lax.psum(partial_bc, "ch")
+    inputs_bc = jnp.sum(lax.all_gather(partial_bc, "ch"), axis=0)
     state_size = decay_rate.shape[0]
     inputs_b = inputs_bc[:, :state_size]
     inputs_r = inputs_bc[:, state_size:]

time: 532 us -> 532 us (level)
  waiting for transfers between devices: 375 us -> 381 us
    psum x1 -> x0, blocking collectives: 34 us -> none  [body(): inputs_bc = lax.psum(partial_bc, 'ch')]
    all_gather x0 -> x1, blocking collectives: none -> 28.7 us  [body(): inputs_bc = jnp.sum(lax.all_gather(partial_bc, 'ch'), axis=0)]
where the time goes in v1:
time: 532 us; the launch traced here: 528 us
  waiting for transfers between devices  381 us (72%)
  other arithmetic  38.7 us (7%)
  starting transfers between devices  34.7 us (7%)
  blocking collectives  28.7 us (5%)
  local copies, waits for them, and re-layouts  24.6 us (5%)
  between operations  13.7 us (3%)
  matrix products  5.68 us (1%)
    all_gather x4, waiting for transfers between devices, carried_in(): gathered = jax.tree.map(lambda a: lax.all_gather(a, axis), part)  258 us
    reduce_scatter x1, waiting for transfers between devices, body(): lax.psum_scatter(summed.astype(jnp.bfloat16), 'ch', scatter_dimension=1,...  43.4 us
    all_gather x1, waiting for transfers between devices, body(): gathered = lax.all_gather(to_gather, 'ch', axis=2, tiled=True)  36.3 us
    ppermute x10, waiting for transfers between devices, from_partner(): return lax.ppermute(block, axis, route)  35.1 us
    ppermute x10, starting transfers between devices, from_partner(): return lax.ppermute(block, axis, route)  32.5 us
    all_gather x1, blocking collectives, body(): inputs_bc = jnp.sum(lax.all_gather(partial_bc, 'ch'), axis=0)  28.7 us
    add x16, other arithmetic, link(): return (before[0] * follow[0], before[1] * follow[0] + follow[1])  13.5 us
  transfers between devices with their start and end apart: 17, of which 17 were waited for; matrix products, arithmetic and copies ran while one was open for 4% of the time, Pallas kernels for 0%

profile of v1, /device:TPU:4, one launch (start us, length us, event | category | flops | bytes accessed | tf_op | source)
XLA Modules:
  0.0 528.3 jit_solution(1955905939545393081)
XLA Ops:
  6.5 1.5 collective-permute-done
  8.0 1.9 collective-permute-start.1
  9.9 2.4 collective-permute-done.1
  12.3 3.3 collective-permute-start.2
  15.6 2.6 collective-permute-done.2
  18.2 7.3 %collective-permute-start.3 = (bf16[128,256]{1,0:T(8,128)(2,1)S(1)}, bf16[128,256]{1,0:T(8,128)(2,1)S(1)}, u32[]{:S(2)}, u32[]{:S(2)}) collective-permute-start(bf16[128,256]{1,0:T(8,128)(2,1)S(1)} %collective-permute-done.2), channel_id=1, source_target_pairs={{0,64},{64,0},{8,72},{72,8},{16,80},{80,16},{24,88},{88,24},{32,96... | collective-permute-start | bytes 196616 | tf_op jit(solution)/shard_map/ppermute | solution.py:17
  25.4 2.3 collective-permute-done.3
  27.7 1.5 collective-permute-start.4
  29.2 4.2 collective-permute-done.4
  33.5 1.5 pad_maximum_fusion.1
  35.0 0.8 copy.31
  36.0 0.7 fusion.192
  36.7 2.6 fusion.187
  39.4 0.7 all-gather.15.cloned.1.call-update
  40.1 0.8 fusion.197
  40.9 0.9 fusion.196
  41.9 0.9 fusion.198
  42.7 36.3 %all-gather.9.cloned.1.call-done = bf16[2,128,2048]{2,1,0:T(8,128)(2,1)} async-done(((bf16[2,128,256]{2,1,0:T(8,128)(2,1)}), bf16[2,128,2048]{2,1,0:T(8,128)(2,1)}) %all-gather.9.cloned.1.call-update) | async-done | bytes 1048592 | tf_op jit(solution)/shard_map/all_gather | solution.py:126
  79.0 1.5 fusion.168
  80.5 2.9 fusion.171
  83.5 1.8 rev.9
  85.3 3.6 convolution_convert_fusion
  89.0 1.9 collective-permute-start.5
  91.0 6.5 %collective-permute-done.5 = bf16[2,3,512]{2,1,0:T(4,128)(2,1)S(1)} collective-permute-done((bf16[2,3,512]{2,1,0:T(4,128)(2,1)S(1)}, bf16[2,3,512]{2,1,0:T(4,128)(2,1)S(1)}, u32[]{:S(2)}, u32[]{:S(2)}) %collective-permute-start.5) | collective-permute-done | bytes 6176 | tf_op jit(solution)/shard_map/ppermute | solution.py:23
  98.1 28.7 %all-gather.1 = f32[16,32,128]{2,1,0:T(8,128)S(1)} all-gather(f32[2,32,128]{2,1,0:T(8,128)S(1)} %convolution_bitcast_fusion), channel_id=3, replica_groups=mesh['seq'=32,'ch'=8] {'ch'}, dimensions={0}, use_global_device_ids=true | all-gather | bytes 294912 | tf_op jit(solution)/shard_map/all_gather | solution.py:152
  127.2 5.1 while.41
  133.8 25.9 %all-gather.17.cloned.1.call-done = f32[512,512]{1,0:T(8,128)} async-done(((f32[16,512]{1,0:T(8,128)}), f32[512,512]{1,0:T(8,128)}) %all-gather.17.cloned.1.call-update) | async-done | bytes 1048592 | tf_op jit(solution)/shard_map/all_gather | solution.py:28
  159.7 77.5 %all-gather.15.cloned.1.call-done = f32[512,512]{1,0:T(8,128)} async-done(((f32[16,512]{1,0:T(8,128)}), f32[512,512]{1,0:T(8,128)}) %all-gather.15.cloned.1.call-update) | async-done | bytes 1048592 | tf_op jit(solution)/shard_map/all_gather | solution.py:28
  237.2 77.3 %all-gather.11.cloned.1.call-done = f32[32,16,512]{2,1,0:T(8,128)} async-done(((f32[1,16,512]{2,1,0:T(8,128)}), f32[32,16,512]{2,1,0:T(8,128)}) %all-gather.11.cloned.1.call-update) | async-done | bytes 1048592 | tf_op jit(solution)/shard_map/all_gather | solution.py:28
  314.5 77.3 %all-gather.13.cloned.1.call-done = f32[32,16,512]{2,1,0:T(8,128)} async-done(((f32[1,16,512]{2,1,0:T(8,128)}), f32[32,16,512]{2,1,0:T(8,128)}) %all-gather.13.cloned.1.call-update) | async-done | bytes 1048592 | tf_op jit(solution)/shard_map/all_gather | solution.py:28
  391.8 13.8 %while.39 = (s32[]{:T(128)}, f32[16,512]{1,0:T(8,128)S(1)}, f32[16,512]{1,0:T(8,128)S(1)}, s32[]{:T(128)}, f32[32,16,512]{2,1,0:T(8,128)}, /*index=5*/f32[32,16,...) while((s32[]{:T(128)}, f32[16,512]{1,0:T(8,128)S(1)}, ...), condition=%wide.region_10.11_spmd, body=%wide.region_9.10_spmd.sunk | while | flops 32773 | bytes 262291 | solution.py:36
  391.8 0.8 bitcast_add_fusion.4
  392.7 0.8 bitcast_add_fusion.4
  393.6 0.8 bitcast_add_fusion.4
  394.4 0.8 bitcast_add_fusion.4
  395.3 0.8 bitcast_add_fusion.4
  396.2 0.8 bitcast_add_fusion.4
  397.0 0.8 bitcast_add_fusion.4
  397.9 0.8 bitcast_add_fusion.4
  398.8 0.8 bitcast_add_fusion.4
  399.6 0.8 bitcast_add_fusion.4
  400.5 0.8 bitcast_add_fusion.4
  401.4 0.8 bitcast_add_fusion.4
  402.2 0.8 bitcast_add_fusion.4
  403.1 0.8 bitcast_add_fusion.4
  403.9 0.8 bitcast_add_fusion.4
  404.8 0.8 bitcast_add_fusion.4
  405.7 16.8 %while.40 = (s32[]{:T(128)}, f32[2,16,512]{2,1,0:T(8,128)S(1)}, f32[8,16,2,512]{3,2,1,0:T(2,128)}, f32[8,16,2]{2,1,0:T(8,128)S(1)}, f32[16,512]{1,0:T(8,128)S(1)...) while((s32[]{:T(128)}, f32[2,16,512]{2,1,0:T(8,128)S(1)}, ...), condition=%wide.region_28.29_spmd, body=%wide.region_11.28_spmd.sunk | while | flops 2818065 | bytes 1473593 | solution.py:94
  407.3 0.6 bitcast_dynamic-update-slice_fusion.2
  417.7 0.6 bitcast_dynamic-update-slice_fusion.2
  422.5 1.2 fusion.182
  423.7 1.2 collective-permute-start.6
  424.9 1.0 collective-permute-done.6
  425.9 2.6 collective-permute-start.7
  428.5 4.0 collective-permute-done.7
  432.5 6.1 %collective-permute-start.8 = (bf16[128,512]{1,0:T(8,128)(2,1)S(1)}, bf16[128,512]{1,0:T(8,128)(2,1)S(1)}, u32[]{:S(2)}, u32[]{:S(2)}) collective-permute-start(bf16[128,512]{1,0:T(8,128)(2,1)S(1)} %collective-permute-done.7), channel_id=1, source_target_pairs={{0,32},{32,0},{8,40},{40,8},{16,48},{48,16},{24,56},{56,24},{64,96... | collective-permute-start | bytes 393224 | tf_op jit(solution)/shard_map/ppermute | solution.py:17
  438.6 6.3 %collective-permute-done.8 = bf16[128,512]{1,0:T(8,128)(2,1)S(1)} collective-permute-done((bf16[128,512]{1,0:T(8,128)(2,1)S(1)}, bf16[128,512]{1,0:T(8,128)(2,1)S(1)}, u32[]{:S(2)}, u32[]{:S(2)}) %collective-permute-start.8) | collective-permute-done | bytes 131104 | tf_op jit(solution)/shard_map/ppermute | solution.py:17
  444.9 8.6 %collective-permute-start.9 = (bf16[128,512]{1,0:T(8,128)(2,1)S(1)}, bf16[128,512]{1,0:T(8,128)(2,1)S(1)}, u32[]{:S(2)}, u32[]{:S(2)}) collective-permute-start(bf16[128,512]{1,0:T(8,128)(2,1)S(1)} %collective-permute-done.8), channel_id=1, source_target_pairs={{0,64},{64,0},{8,72},{72,8},{16,80},{80,16},{24,88},{88,24},{32,96... | collective-permute-start | bytes 393224 | tf_op jit(solution)/shard_map/ppermute | solution.py:17
  453.5 4.9 collective-permute-done.9
  458.9 6.0 %collective-permute-done.10 = bf16[128,512]{1,0:T(8,128)(2,1)S(1)} collective-permute-done((bf16[128,512]{1,0:T(8,128)(2,1)S(1)}, bf16[128,512]{1,0:T(8,128)(2,1)S(1)}, u32[]{:S(2)}, u32[]{:S(2)}) %collective-permute-start.10) | collective-permute-done | bytes 131104 | tf_op jit(solution)/shard_map/ppermute | solution.py:17
  465.1 1.5 fusion.199
  466.6 9.3 %rev.11 = f32[128,2048]{1,0:T(8,128)} reverse(f32[128,2048]{1,0:T(8,128)} %fusion.199), dimensions={1} | reverse | bytes 2097152 | tf_op jit(solution)/shard_map/rev | solution.py:188
  475.9 2.1 add_convert_fusion
  478.1 43.4 %reduce-scatter.2.cloned.1.call-done = bf16[128,256]{1,0:T(8,128)(2,1)} async-done(((bf16[128,2048]{1,0:T(8,128)(2,1)}), bf16[128,256]{1,0:T(8,128)(2,1)}) %reduce-scatter.2.cloned.1.call-update) | async-done | bytes 65552 | tf_op jit(solution)/shard_map/reduce_scatter | solution.py:190
  (279 shorter events, 22.9 us)
Async XLA Ops:
  6.5 451.9 %copy-start = (bf16[512,2048]{1,0:T(8,128)(2,1)S(1)}, bf16[512,2048]{1,0:T(8,128)(2,1)}, u32[]{:S(2)}) copy-start(bf16[512,2048]{1,0:T(8,128)(2,1)} %param.29) | copy-start | bytes 6291460
  6.5 72.5 %all-gather.9.cloned.1.call-start = ((), (), s32[]{:S(2)}) async-start(), calls=%async_computation.1 | async-start | bytes 1179648 | tf_op jit(solution)/shard_map/all_gather | solution.py:126
  6.5 1.5 collective-permute-start
  8.0 4.3 collective-permute-start.1
  12.3 5.8 %collective-permute-start.2 = (bf16[128,256]{1,0:T(8,128)(2,1)S(1)}, bf16[128,256]{1,0:T(8,128)(2,1)S(1)}, u32[]{:S(2)}, u32[]{:S(2)}) collective-permute-start(bf16[128,256]{1,0:T(8,128)(2,1)S(1)} %collective-permute-done.1), channel_id=1, source_target_pairs={{0,32},{32,0},{8,40},{40,8},{16,48},{48,16},{24,56},{56,24},{64,96... | collective-permute-start | bytes 196616 | tf_op jit(solution)/shard_map/ppermute | solution.py:17
  18.2 9.5 %collective-permute-start.3 = (bf16[128,256]{1,0:T(8,128)(2,1)S(1)}, bf16[128,256]{1,0:T(8,128)(2,1)S(1)}, u32[]{:S(2)}, u32[]{:S(2)}) collective-permute-start(bf16[128,256]{1,0:T(8,128)(2,1)S(1)} %collective-permute-done.2), channel_id=1, source_target_pairs={{0,64},{64,0},{8,72},{72,8},{16,80},{80,16},{24,88},{88,24},{32,96... | collective-permute-start | bytes 196616 | tf_op jit(solution)/shard_map/ppermute | solution.py:17
  27.7 5.8 %collective-permute-start.4 = (bf16[128,256]{1,0:T(8,128)(2,1)S(1)}, bf16[128,256]{1,0:T(8,128)(2,1)S(1)}, u32[]{:S(2)}, u32[]{:S(2)}) collective-permute-start(bf16[128,256]{1,0:T(8,128)(2,1)S(1)} %collective-permute-done.3), channel_id=1, source_target_pairs={{0,128},{128,0},{8,136},{136,8},{16,144},{144,16},{24,152},{152,24... | collective-permute-start | bytes 196616 | tf_op jit(solution)/shard_map/ppermute | solution.py:17
  35.0 124.7 %all-gather.17.cloned.1.call-start = ((), (), s32[]{:S(2)}) async-start(), calls=%async_computation.6 | async-start | bytes 1081344 | tf_op jit(solution)/shard_map/all_gather | solution.py:28
  39.3 197.9 %all-gather.15.cloned.1.call-start = ((), (), s32[]{:S(2)}) async-start(), calls=%async_computation.5 | async-start | bytes 1081344 | tf_op jit(solution)/shard_map/all_gather | solution.py:28
  40.1 274.4 %all-gather.11.cloned.1.call-start = ((), (), s32[]{:S(2)}) async-start(), calls=%async_computation.2 | async-start | bytes 1081344 | tf_op jit(solution)/shard_map/all_gather | solution.py:28
  85.3 12.3 %copy-start.2 = (f32[512]{0:T(512)S(1)}, f32[512]{0:T(512)}, u32[]{:S(2)}) copy-start(f32[512]{0:T(512)} %param.25) | copy-start | bytes 6148
  85.3 12.6 %copy-start.1 = (bf16[32,512]{1,0:T(8,128)(2,1)S(1)}, bf16[32,512]{1,0:T(8,128)(2,1)}, u32[]{:S(2)}) copy-start(bf16[32,512]{1,0:T(8,128)(2,1)} %param.26) | copy-start | bytes 98308
  89.0 8.6 %collective-permute-start.5 = (bf16[2,3,512]{2,1,0:T(4,128)(2,1)S(1)}, bf16[2,3,512]{2,1,0:T(4,128)(2,1)S(1)}, u32[]{:S(2)}, u32[]{:S(2)}) collective-permute-start(bf16[2,3,512]{2,1,0:T(4,128)(2,1)S(1)} %slice.623), channel_id=1, source_target_pairs={{0,8},{8,16},{16,24},{24,32},{32,40},{40,48},{48,56},{56,64},{64,7... | collective-permute-start | bytes 18440 | tf_op jit(solution)/shard_map/ppermute | solution.py:23
  133.0 258.8 %all-gather.13.cloned.1.call-start = ((), (), s32[]{:S(2)}) async-start(), calls=%async_computation.3 | async-start | bytes 1081344 | tf_op jit(solution)/shard_map/all_gather | solution.py:28
  133.6 387.9 %reduce-scatter.2.cloned.1.call-start = ((), (), s32[]{:S(2)}) async-start(), calls=%async_computation.4 | async-start | bytes 589824 | tf_op jit(solution)/shard_map/reduce_scatter | solution.py:190
  405.7 16.8 %copy-start.3 = (f32[512]{0:T(512)S(1)}, f32[512]{0:T(512)}, u32[]{:S(2)}) copy-start(f32[512]{0:T(512)} %param.28) | copy-start | bytes 6148
  423.7 2.2 collective-permute-start.6
  425.9 6.7 %collective-permute-start.7 = (bf16[128,512]{1,0:T(8,128)(2,1)S(1)}, bf16[128,512]{1,0:T(8,128)(2,1)S(1)}, u32[]{:S(2)}, u32[]{:S(2)}) collective-permute-start(bf16[128,512]{1,0:T(8,128)(2,1)S(1)} %collective-permute-done.6), channel_id=1, source_target_pairs={{0,16},{16,0},{8,24},{24,8},{32,48},{48,32},{40,56},{56,40},{64,80... | collective-permute-start | bytes 393224 | tf_op jit(solution)/shard_map/ppermute | solution.py:17
  432.5 12.4 %collective-permute-start.8 = (bf16[128,512]{1,0:T(8,128)(2,1)S(1)}, bf16[128,512]{1,0:T(8,128)(2,1)S(1)}, u32[]{:S(2)}, u32[]{:S(2)}) collective-permute-start(bf16[128,512]{1,0:T(8,128)(2,1)S(1)} %collective-permute-done.7), channel_id=1, source_target_pairs={{0,32},{32,0},{8,40},{40,8},{16,48},{48,16},{24,56},{56,24},{64,96... | collective-permute-start | bytes 393224 | tf_op jit(solution)/shard_map/ppermute | solution.py:17
  444.9 13.5 %collective-permute-start.9 = (bf16[128,512]{1,0:T(8,128)(2,1)S(1)}, bf16[128,512]{1,0:T(8,128)(2,1)S(1)}, u32[]{:S(2)}, u32[]{:S(2)}) collective-permute-start(bf16[128,512]{1,0:T(8,128)(2,1)S(1)} %collective-permute-done.8), channel_id=1, source_target_pairs={{0,64},{64,0},{8,72},{72,8},{16,80},{80,16},{24,88},{88,24},{32,96... | collective-permute-start | bytes 393224 | tf_op jit(solution)/shard_map/ppermute | solution.py:17
  458.4 6.5 %collective-permute-start.10 = (bf16[128,512]{1,0:T(8,128)(2,1)S(1)}, bf16[128,512]{1,0:T(8,128)(2,1)S(1)}, u32[]{:S(2)}, u32[]{:S(2)}) collective-permute-start(bf16[128,512]{1,0:T(8,128)(2,1)S(1)} %collective-permute-done.9), channel_id=1, source_target_pairs={{0,128},{128,0},{8,136},{136,8},{16,144},{144,16},{24,152},{152,24... | collective-permute-start | bytes 393224 | tf_op jit(solution)/shard_map/ppermute | solution.py:17
Sparse Core Ops, SparseCore 0:
  35.1 43.8 all-gather.8
  81.8 77.8 all-gather.16
  162.5 74.6 all-gather.14
  239.8 74.5 all-gather.10
  317.1 74.6 all-gather.12
  478.2 43.2 reduce-scatter.1
